TPU v7x, 1024 devices: a whole 8x8x8 slice. The times are simulated.
1024 devices in a mesh: row: 128 (over z, x, core), col: 8 (over y).
Axes of the slice: x: 8, y: 8, z: 8, core: 2. Of those that a mesh axis runs over, the one named last changes fastest.
Arguments:
- deposit_maps: float32 [16384, 8192], P('row', 'col'), may hold values from -30 to 30, as said below
- test_matrix: float32 [8192, 256], P('col'), may hold values from -1 to 1
Outputs:
- scaled_basis: float32 [16384, 256], P('row')
- projected: float32 [256, 8192], P('row', 'col')
Inputs may be any that keep to these rules, and one draw needn't show every extreme that they name: `deposit_maps`: a dense real matrix.
All inputs are finite; a program needn't handle non-finite values.
Results may differ from a plain program's by a relative error of at most 0.0003.
Values sent between devices are 32-bit elements; how exact they have to be, the bound alone decides.
No kernel may reach another device: no remote copies, remote signals or barrier semaphores. Data moves between devices by JAX's collectives and lax.ppermute only.
A program may use at most 32 MiB of HBM per device.

v0:
```python
import math

import jax
import jax.numpy as jnp
from jax import lax
from jax.sharding import PartitionSpec as P


def apply_factor(current, gram_matrix):
    lower_factor = jnp.linalg.cholesky(gram_matrix)
    identity = jnp.eye(gram_matrix.shape[0], dtype=jnp.float32)
    inverse = jax.scipy.linalg.solve_triangular(lower_factor, identity, lower=True)
    return jnp.dot(
        current, inverse.T, preferred_element_type=jnp.float32, precision=lax.Precision.HIGHEST
    )


def local_gram(current):
    return jnp.dot(
        current.T, current, preferred_element_type=jnp.float32, precision=lax.Precision.HIGHEST
    )


def passes_rows(current):
    for sweep_index in range(2):
        gram_matrix = lax.psum(local_gram(current), "row")
        current = apply_factor(current, gram_matrix)
    return current


def on_device(deposit_maps, test_matrix):
    partial_sketch = jnp.dot(
        deposit_maps,
        test_matrix,
        preferred_element_type=jnp.float32,
        precision=lax.Precision.HIGHEST,
    )
    sketch = lax.psum(partial_sketch, "col")
    orthonormal = passes_rows(sketch)
    total_rows = orthonormal.shape[0] * lax.axis_size("row")
    scaled_basis = orthonormal * math.sqrt(total_rows)
    projected = lax.psum_scatter(
        jnp.dot(
            orthonormal.T,
            deposit_maps,
            preferred_element_type=jnp.float32,
            precision=lax.Precision.HIGHEST,
        ),
        "row",
        scatter_dimension=0,
        tiled=True,
    )
    return (scaled_basis, projected)


def solution(mesh):
    placed = (P("row", "col"), P("col", None))
    return jax.shard_map(
        on_device,
        mesh=mesh,
        in_specs=placed,
        out_specs=(P("row", None), P("row", "col")),
        check_vma=False,
    )
```

profile of v0, /device:TPU:1, one launch (start us, length us, event | category | flops | bytes accessed | tf_op | source)
XLA Modules:
  0.0 864.6 jit_solution(1508669049545215742)
XLA Ops:
  7.2 0.0 copy-start
  7.2 0.0 all-reduce.7.cloned.1.call-start
  7.2 1.2 copy-done
  8.4 2.3 fusion.29
  10.7 0.0 all-reduce.7.cloned.1.call-update
  10.8 0.0 all-reduce.9.cloned.1.call-start
  10.8 91.2 %all-reduce.7.cloned.1.call-done = f32[128,256]{1,0:T(8,128)} async-done(((f32[128,256]{1,0:T(8,128)}), f32[128,256]{1,0:T(8,128)}) %all-reduce.7.cloned.1.call-update) | async-done | bytes 131088 | tf_op jit(solution)/shard_map/psum | solution.py:38
  102.0 2.1 fusion.30
  104.1 0.0 all-reduce.9.cloned.1.call-update
  104.1 0.0 all-reduce.11.cloned.1.call-start
  104.2 210.6 %all-reduce.9.cloned.1.call-done = f32[256,256]{0,1:T(8,128)} async-done(((f32[256,256]{0,1:T(8,128)}), f32[256,256]{0,1:T(8,128)}) %all-reduce.9.cloned.1.call-update) | async-done | bytes 262160 | tf_op jit(solution)/shard_map/psum | solution.py:26
  314.8 0.0 copy-start.3
  314.8 1.1 copy.9
  316.0 0.0 copy-done.3
  316.0 11.7 %cholesky.130 = f32[128,128]{1,0:T(8,128)S(1)} custom-call(f32[128,128]{1,0:T(8,128)S(1)} %cholesky.194), custom_call_target="Cholesky" | custom-call | tf_op jit(solution)/shard_map/jit(cholesky)/cholesky | solution.py:10
  327.8 9.8 %custom-call.13 = f32[1,128,128]{1,2,0:T(8,128)S(1)} custom-call(f32[1,128,128]{2,1,0:T(8,128)S(1)} %get-tuple-element.47), custom_call_target="InvertDiagBlocksLowerTriangular" | custom-call | tf_op jit(solution)/shard_map/jit(cholesky)/cholesky | solution.py:10
  337.6 0.2 constant_dynamic-update-slice_fusion.3
  337.8 0.3 convolution_subtract_fusion.3
  338.1 11.7 %cholesky.147 = f32[128,128]{1,0:T(8,128)S(1)} custom-call(f32[128,128]{1,0:T(8,128)S(1)} %convolution_subtract_fusion.3), custom_call_target="Cholesky" | custom-call | tf_op jit(solution)/shard_map/jit(cholesky)/cholesky | solution.py:10
  349.9 0.7 compare_reduce_fusion.2
  351.9 0.1 triangular_solve.75
  352.0 4.3 while.4
  352.2 0.7 fusion.53
  352.8 1.3 bitcast_dynamic-update-slice_fusion.4
  354.2 0.7 fusion.53
  354.9 1.3 bitcast_dynamic-update-slice_fusion.4
  356.2 19.7 %custom-call.14 = f32[2,128,128]{1,2,0:T(8,128)S(1)} custom-call(f32[2,128,128]{2,1,0:T(8,128)S(1)} %get-tuple-element.18), custom_call_target="InvertDiagBlocksLowerTriangular" | custom-call | tf_op jit(solution)/shard_map/jit(_solve_triangular)/triangular_solve | solution.py:12
  375.9 0.3 fusion.13
  376.2 0.3 convolution_subtract_fusion.1
  376.5 0.0 copy-start.2
  376.5 0.3 fusion.20
  376.8 0.6 copy-done.2
  377.4 0.4 fusion
  377.8 1.1 fusion.31
  378.9 0.0 all-reduce.11.cloned.1.call-update
  378.9 0.0 all-reduce.13.cloned.1.call-start
  379.0 203.5 %all-reduce.11.cloned.1.call-done = f32[256,256]{0,1:T(8,128)} async-done(((f32[256,256]{0,1:T(8,128)}), f32[256,256]{0,1:T(8,128)}) %all-reduce.11.cloned.1.call-update) | async-done | bytes 262160 | tf_op jit(solution)/shard_map/psum | solution.py:26
  582.5 0.0 copy-start.4
  582.5 1.1 copy.11
  583.7 0.0 copy-done.4
  583.7 11.7 %cholesky.164 = f32[128,128]{1,0:T(8,128)S(1)} custom-call(f32[128,128]{1,0:T(8,128)S(1)} %cholesky.197), custom_call_target="Cholesky" | custom-call | tf_op jit(solution)/shard_map/jit(cholesky)/cholesky | solution.py:10
  595.5 9.8 %custom-call.15 = f32[1,128,128]{1,2,0:T(8,128)S(1)} custom-call(f32[1,128,128]{2,1,0:T(8,128)S(1)} %get-tuple-element.43), custom_call_target="InvertDiagBlocksLowerTriangular" | custom-call | tf_op jit(solution)/shard_map/jit(cholesky)/cholesky | solution.py:10
  605.3 0.2 constant_dynamic-update-slice_fusion.1
  605.5 0.3 convolution_subtract_fusion.2
  605.8 11.7 %cholesky.181 = f32[128,128]{1,0:T(8,128)S(1)} custom-call(f32[128,128]{1,0:T(8,128)S(1)} %convolution_subtract_fusion.2), custom_call_target="Cholesky" | custom-call | tf_op jit(solution)/shard_map/jit(cholesky)/cholesky | solution.py:10
  617.5 0.6 compare_reduce_fusion.1
  618.2 0.7 compare_reduce_fusion
  620.3 4.3 while.5
  620.5 0.6 fusion.54
  621.1 1.4 bitcast_dynamic-update-slice_fusion.5
  622.6 0.6 fusion.54
  623.2 1.4 bitcast_dynamic-update-slice_fusion.5
  624.6 19.7 %custom-call.16 = f32[2,128,128]{1,2,0:T(8,128)S(1)} custom-call(f32[2,128,128]{2,1,0:T(8,128)S(1)} %get-tuple-element.19), custom_call_target="InvertDiagBlocksLowerTriangular" | custom-call | tf_op jit(solution)/shard_map/jit(_solve_triangular)/triangular_solve | solution.py:12
  644.3 0.3 fusion.11
  644.6 0.3 convolution_subtract_fusion
  644.9 0.0 copy-start.1
  644.9 0.3 fusion.16
  645.2 1.1 broadcast_multiply_fusion
  646.3 0.0 copy-done.1
  646.3 2.1 fusion.32
  648.4 0.0 all-reduce.13.cloned.1.call-update
  648.4 1.3 dynamic-slice.5
  650.3 206.4 %all-reduce.13.cloned.1.call-done = f32[256,1024]{1,0:T(8,128)} async-done(((f32[256,1024]{1,0:T(8,128)}), f32[256,1024]{1,0:T(8,128)}) %all-reduce.13.cloned.1.call-update) | async-done | bytes 1048592
  856.7 1.4 constant_dynamic-slice_fusion.2
  (20 shorter events, 0.4 us)
Async XLA Ops:
  7.2 1.2 copy-start
  7.2 94.8 %all-reduce.7.cloned.1.call-start = ((), (), s32[]{:S(2)}) async-start(), calls=%async_computation | async-start | bytes 262144 | tf_op jit(solution)/shard_map/psum | solution.py:38
  10.8 304.1 %all-reduce.9.cloned.1.call-start = ((), (), s32[]{:S(2)}) async-start(), calls=%async_computation.1 | async-start | bytes 524288 | tf_op jit(solution)/shard_map/psum | solution.py:26
  104.1 478.3 %all-reduce.11.cloned.1.call-start = ((), (), s32[]{:S(2)}) async-start(), calls=%async_computation.2 | async-start | bytes 524288 | tf_op jit(solution)/shard_map/psum | solution.py:26
  314.8 1.2 copy-start.3
  376.5 0.9 copy-start.2
  378.9 477.7 %all-reduce.13.cloned.1.call-start = ((), (), s32[]{:S(2)}) async-start(), calls=%async_computation.3 | async-start | bytes 2097152
  582.5 1.2 copy-start.4
  644.9 1.4 copy-start.1
Sparse Core Ops, SparseCore 0:
  10.9 91.1 all-reduce.6
  105.2 209.5 all-reduce.8
  379.1 203.3 all-reduce.10
  648.5 208.1 all-reduce.12
where the time goes:
time: 866 us; the launch traced here: 865 us
  waiting for transfers between devices  712 us (82%)
  other arithmetic  108 us (12%)
  between operations  17.3 us (2%)
  local copies, waits for them, and re-layouts  14.9 us (2%)
  matrix products  11.8 us (1%)
    psum x2, waiting for transfers between devices, passes_rows(): gram_matrix = lax.psum(local_gram(current), 'row')  414 us
    unnamed x5, waiting for transfers between devices  206 us
    psum x1, waiting for transfers between devices, on_device(): sketch = lax.psum(partial_sketch, 'col')  91.2 us
    another operation x13, other arithmetic, apply_factor(): lower_factor = jnp.linalg.cholesky(gram_matrix)  68.7 us
    another operation x5, other arithmetic, apply_factor(): jax.scipy.linalg.solve_triangular(lower_factor, identity, lower=True)  39.4 us
  transfers between devices with their start and end apart: 4, of which 4 were waited for; matrix products, arithmetic and copies ran while one was open for 0% of the time, Pallas kernels for 0%

commit v1 on v0

v1 whole, which is shorter than its diff:
```python
import math

import jax
import jax.numpy as jnp
from jax import lax
from jax.experimental import pallas as pl
from jax.experimental.pallas import tpu as pltpu
from jax.sharding import Mesh
from jax.sharding import PartitionSpec as P

HIGHEST = lax.Precision.HIGHEST

def invert_small(block):
    lanes = 128
    size = block.shape[0]
    entry = [[jnp.broadcast_to(block[i:i+1, j:j+1], (8, lanes)) for j in range(i + 1)] for i in range(size)]
    recip = []
    lower = [[None] * size for _ in range(size)]
    for j in range(size):
        r = lax.rsqrt(entry[j][j])
        recip.append(r)
        for i in range(j + 1, size):
            lower[i][j] = entry[i][j] * r
        for i in range(j + 1, size):
            for m in range(j + 1, i + 1):
                entry[i][m] = entry[i][m] - lower[i][j] * lower[m][j]
    inv = [[None] * size for _ in range(size)]
    for j in range(size):
        inv[j][j] = recip[j]
        for i in range(j + 1, size):
            total = lower[i][j] * inv[j][j]
            for m in range(j + 1, i):
                total = total + lower[i][m] * inv[m][j]
            inv[i][j] = -(recip[i] * total)
    return inv

def wide(x, width):
    return jnp.concatenate([x] * (width // 128), axis=1)

def factor_kernel(g_ref, w_ref, m_ref):
    n = 256
    width = 384
    row = lax.broadcasted_iota(jnp.int32, (n, n), 0)
    col = lax.broadcasted_iota(jnp.int32, (n, n), 1)
    m_ref[:, :n] = g_ref[...]
    m_ref[:, n:] = jnp.where(row == col, 1.0, 0.0).astype(jnp.float32)
    sub = lax.broadcasted_iota(jnp.int32, (8, 128), 0)
    zero = jnp.zeros((8, 128), jnp.float32)
    for half in range(2):
        base = 128 * half
        cols = slice(base, base + width)
        for p in range(16):
            k = base + 8 * p
            rows = m_ref[k:k+8, cols]
            inv = invert_small(rows[:, 8*p:8*p+8])
            panel = None
            for j in range(8):
                coef = zero
                for i in range(j, 8):
                    coef = jnp.where(sub == i, inv[i][j], coef)
                term = wide(coef, width) * jnp.broadcast_to(rows[j:j+1, :], (8, width))
                panel = term if panel is None else panel + term
            m_ref[k:k+8, cols] = panel
            if p == 15:
                continue
            solved = None
            for j in range(8):
                coef = zero
                for m in range(j + 1):
                    coef = jnp.where(sub == m, inv[j][m], coef)
                term = wide(coef, width) * jnp.broadcast_to(panel[j:j+1, :], (8, width))
                solved = term if solved is None else solved + term
            spread = [jnp.broadcast_to(solved[m:m+1, :], (8, width)) for m in range(8)]
            for rb in range(p + 1, 16):
                i = base + 8 * rb
                left = m_ref[i:i+8, k:k+8]
                acc = m_ref[i:i+8, cols]
                for m in range(8):
                    acc = acc - wide(jnp.broadcast_to(left[:, m:m+1], (8, 128)), width) * spread[m]
                m_ref[i:i+8, cols] = acc
        if half == 0:
            top = m_ref[0:128, 128:384]
            left = m_ref[0:128, 128:256].T
            m_ref[128:256, 128:384] = m_ref[128:256, 128:384] - jnp.dot(
                left, top, preferred_element_type=jnp.float32, precision=lax.Precision.HIGHEST)
    w_ref[...] = m_ref[:, n:]


def factor(gram_matrix):
    return pl.pallas_call(
        factor_kernel,
        out_shape=jax.ShapeDtypeStruct((256, 256), jnp.float32),
        in_specs=[pl.BlockSpec(memory_space=pltpu.VMEM)],
        out_specs=pl.BlockSpec(memory_space=pltpu.VMEM),
        scratch_shapes=[pltpu.VMEM((256, 512), jnp.float32)],
        name="factor",
    )(gram_matrix)


def dot(left, right, contract):
    return lax.dot_general(
        left, right, ((contract[:1], contract[1:]), ((), ())), precision=HIGHEST, preferred_element_type=jnp.float32
    )


def scatter_sum(parts, axes):
    return jnp.sum(lax.all_to_all(parts, axes, 0, 0, tiled=True), axis=0)


def spread(part, axes, count):
    return lax.all_to_all(jnp.broadcast_to(part[None], (count, *part.shape)), axes, 0, 0, tiled=True)


def sum_rows(gram_matrix):
    other = lax.ppermute(gram_matrix, "core", [(0, 1), (1, 0)])
    chip_sum = gram_matrix + other
    part = scatter_sum(chip_sum.reshape(64, 8, 128), ("z", "x"))
    return spread(part, ("z", "x"), 64).reshape(256, 256)


def on_device(deposit_maps, test_matrix):
    partial_sketch = dot(deposit_maps, test_matrix, (1, 0))
    part = scatter_sum(partial_sketch.reshape(8, 16, 256), "col")
    current = spread(part, "col", 8).reshape(128, 256)
    for sweep_index in range(2):
        inverse = factor(sum_rows(dot(current, current, (0, 0))))
        current = dot(current, inverse, (1, 1))
    total_rows = current.shape[0] * 128
    scaled_basis = current * math.sqrt(total_rows)
    projected = dot(current, deposit_maps, (0, 0))
    projected = scatter_sum(projected.reshape(128, 2, 1024), ("z", "x", "core"))
    return (scaled_basis, projected)


def solution(mesh):
    chips = Mesh(mesh.devices.reshape(8, 8, 2, 8), ("z", "x", "core", "col"))
    rows = ("z", "x", "core")
    return jax.shard_map(
        on_device,
        mesh=chips,
        in_specs=(P(rows, "col"), P("col", None)),
        out_specs=(P(rows, None), P(rows, "col")),
        check_vma=False,
    )
```

time: 866 us -> 202 us (0.23)
  waiting for transfers between devices: 712 us -> 2.28 us
  blocking collectives: 0 us -> 145 us
  other arithmetic: 108 us -> 1.21 us
  Pallas kernels: 0 us -> 23.4 us
  starting transfers between devices: 0.16 us -> 18.2 us
  between operations: 17.3 us -> 0.75 us
  local copies, waits for them, and re-layouts: 14.9 us -> 3.47 us
    psum x3 -> x0, waiting for transfers between devices: 505 us -> none  [the longest x2 414 us: passes_rows(): gram_matrix = lax.psum(local_gram(current), 'row')]
    unnamed x5 -> x0, waiting for transfers between devices: 206 us -> none
    all_to_all x0 -> x7, blocking collectives: none -> 145 us  [the longest x4 99.8 us: scatter_sum(): return jnp.sum(lax.all_to_all(parts, axes, 0, 0, tiled=True), axis=0)]
    another operation x18 -> x0, other arithmetic: 108 us -> none  [the longest x13 68.7 us: apply_factor(): lower_factor = jnp.linalg.cholesky(gram_matrix)]
    pallas_call x0 -> x2, Pallas kernels: none -> 23.4 us  [factor(): pl.pallas_call(factor_kernel, out_shape=jax.ShapeDtypeStruct((256, 256),...]
    ppermute x0 -> x2, starting transfers between devices: none -> 18.2 us  [sum_rows(): other = lax.ppermute(gram_matrix, 'core', [(0, 1), (1, 0)])]
  transfers between devices with their start and end apart: 4 -> 2, of which waited for: 4 -> 2; matrix products, arithmetic and copies ran while one was open for 0% -> 0% of each run, Pallas kernels for 0% -> 0%
where the time goes in v1:
time: 202 us; the launch traced here: 201 us
  blocking collectives  145 us (72%)
  Pallas kernels  23.4 us (12%)
  starting transfers between devices  18.2 us (9%)
  matrix products  6.88 us (3%)
  local copies, waits for them, and re-layouts  3.47 us (2%)
  waiting for transfers between devices  2.28 us (1%)
    all_to_all x4, blocking collectives, scatter_sum(): return jnp.sum(lax.all_to_all(parts, axes, 0, 0, tiled=True), axis=0)  99.8 us
    all_to_all x3, blocking collectives, spread(): lax.all_to_all(jnp.broadcast_to(part[None], (count, *part.shape)), axes,...  45.5 us
    pallas_call x2, Pallas kernels, factor(): pl.pallas_call(factor_kernel, out_shape=jax.ShapeDtypeStruct((256, 256),...  23.4 us
    ppermute x2, starting transfers between devices, sum_rows(): other = lax.ppermute(gram_matrix, 'core', [(0, 1), (1, 0)])  18.2 us
    dot_general x6, matrix products, dot(): lax.dot_general(left, right, ((contract[:1], contract[1:]), ((), ())), pr...  6.88 us
  transfers between devices with their start and end apart: 2, of which 2 were waited for; matrix products, arithmetic and copies ran while one was open for 0% of the time, Pallas kernels for 0%

profile of v1, /device:TPU:1, one launch (start us, length us, event | category | flops | bytes accessed | tf_op | source)
XLA Modules:
  0.0 201.5 jit_solution(11530198734750673716)
XLA Ops:
  0.6 0.0 copy-start
  0.6 1.2 copy-done
  1.9 1.7 fusion
  3.5 15.8 %all_to_all.35 = f32[8,16,256]{2,1,0:T(8,128)S(1)} all-to-all(f32[8,16,256]{2,1,0:T(8,128)S(1)} %bitcast.17), channel_id=1, replica_groups=mesh['z'=8,'x'=8,'core'=2,'col'=8] {'col'}, dimensions={0} | all-to-all | bytes 262144 | tf_op jit(solution)/shard_map/all_to_all | solution.py:107
  19.4 10.4 %all_to_all.36 = f32[8,16,256]{2,1,0:T(8,128)S(1)} all-to-all(f32[8,16,256]{2,1,0:T(8,128)S(1)} %broadcast_in_dim.6), channel_id=1, replica_groups=mesh['z'=8,'x'=8,'core'=2,'col'=8] {'col'}, dimensions={0} | all-to-all | bytes 262144 | tf_op jit(solution)/shard_map/all_to_all | solution.py:111
  29.8 0.4 convolution_bitcast_fusion
  30.3 12.7 %collective-permute-start = (f32[256,256]{1,0:T(8,128)S(1)}, f32[256,256]{1,0:T(8,128)S(1)}, u32[]{:S(2)}, u32[]{:S(2)}) collective-permute-start(f32[256,256]{1,0:T(8,128)S(1)} %convolution_bitcast_fusion), channel_id=1, source_target_pairs={{0,8},{8,0},{1,9},{9,1},{2,10},{10,2},{3,11},{11,3},{4,12},{12,4},... | collective-permute-start | bytes 786440 | tf_op jit(solution)/shard_map/ppermute | solution.py:115
  43.0 1.1 collective-permute-done
  44.2 27.7 %all_to_all.37 = f32[64,8,128]{2,1,0:T(8,128)S(1)} all-to-all(f32[64,8,128]{2,1,0:T(8,128)S(1)} %reshape.30), channel_id=1, replica_groups=mesh['z'=8,'x'=8,'core'=2,'col'=8] {'z','x'}, dimensions={0} | all-to-all | bytes 524288 | tf_op jit(solution)/shard_map/all_to_all | solution.py:107
  71.9 0.1 reduce_sum.37
  72.0 17.7 %all_to_all.38 = f32[64,8,128]{2,1,0:T(8,128)S(1)} all-to-all(f32[64,8,128]{2,1,0:T(8,128)S(1)} %broadcast_in_dim.7), channel_id=1, replica_groups=mesh['z'=8,'x'=8,'core'=2,'col'=8] {'z','x'}, dimensions={0} | all-to-all | bytes 524288 | tf_op jit(solution)/shard_map/all_to_all | solution.py:111
  89.6 0.8 reshape.31.g_ref
  90.4 11.7 %factor.2 = f32[256,256]{1,0:T(8,128)} custom-call(f32[256,256]{1,0:T(8,128)} %reshape.31.g_ref), custom_call_target="tpu_custom_call" | custom-call | tf_op jit(solution)/shard_map/factor/pallas_call | solution.py:90
  102.1 1.3 fusion.1
  103.4 0.4 fusion.2
  103.8 5.4 %collective-permute-start.1 = (f32[256,256]{1,0:T(8,128)S(1)}, f32[256,256]{1,0:T(8,128)S(1)}, u32[]{:S(2)}, u32[]{:S(2)}) collective-permute-start(f32[256,256]{1,0:T(8,128)S(1)} %fusion.2), channel_id=1, source_target_pairs={{0,8},{8,0},{1,9},{9,1},{2,10},{10,2},{3,11},{11,3},{4,12},{12,4},... | collective-permute-start | bytes 786440 | tf_op jit(solution)/shard_map/ppermute | solution.py:115
  109.3 1.1 collective-permute-done.1
  110.5 17.2 %all_to_all.39 = f32[64,8,128]{2,1,0:T(8,128)S(1)} all-to-all(f32[64,8,128]{2,1,0:T(8,128)S(1)} %reshape.32), channel_id=1, replica_groups=mesh['z'=8,'x'=8,'core'=2,'col'=8] {'z','x'}, dimensions={0} | all-to-all | bytes 524288 | tf_op jit(solution)/shard_map/all_to_all | solution.py:107
  127.7 0.1 reduce_sum.38
  127.8 17.4 %all_to_all.40 = f32[64,8,128]{2,1,0:T(8,128)S(1)} all-to-all(f32[64,8,128]{2,1,0:T(8,128)S(1)} %broadcast_in_dim.8), channel_id=1, replica_groups=mesh['z'=8,'x'=8,'core'=2,'col'=8] {'z','x'}, dimensions={0} | all-to-all | bytes 524288 | tf_op jit(solution)/shard_map/all_to_all | solution.py:111
  145.2 0.8 reshape.33.g_ref
  146.0 0.0 copy-start.1
  146.0 11.7 %factor.3 = f32[256,256]{1,0:T(8,128)} custom-call(f32[256,256]{1,0:T(8,128)} %reshape.33.g_ref), custom_call_target="tpu_custom_call" | custom-call | tf_op jit(solution)/shard_map/factor/pallas_call | solution.py:90
  157.7 2.0 broadcast_multiply_fusion
  159.7 0.0 copy-done.1
  159.7 1.0 fusion.3
  160.7 0.6 reshape.34
  161.4 39.1 %all_to_all.41 = f32[128,2,1024]{2,1,0:T(2,128)S(1)} all-to-all(f32[128,2,1024]{2,1,0:T(2,128)S(1)} %reshape.34), channel_id=1, replica_groups=mesh['z'=8,'x'=8,'core'=2,'col'=8] {'z','x','core'}, dimensions={0} | all-to-all | bytes 2097152 | tf_op jit(solution)/shard_map/all_to_all | solution.py:107
  200.5 1.0 reduce_sum.39
  (8 shorter events, 0.2 us)
Async XLA Ops:
  0.6 1.2 copy-start
  30.3 13.9 %collective-permute-start = (f32[256,256]{1,0:T(8,128)S(1)}, f32[256,256]{1,0:T(8,128)S(1)}, u32[]{:S(2)}, u32[]{:S(2)}) collective-permute-start(f32[256,256]{1,0:T(8,128)S(1)} %convolution_bitcast_fusion), channel_id=1, source_target_pairs={{0,8},{8,0},{1,9},{9,1},{2,10},{10,2},{3,11},{11,3},{4,12},{12,4},... | collective-permute-start | bytes 786440 | tf_op jit(solution)/shard_map/ppermute | solution.py:115
  103.8 6.6 %collective-permute-start.1 = (f32[256,256]{1,0:T(8,128)S(1)}, f32[256,256]{1,0:T(8,128)S(1)}, u32[]{:S(2)}, u32[]{:S(2)}) collective-permute-start(f32[256,256]{1,0:T(8,128)S(1)} %fusion.2), channel_id=1, source_target_pairs={{0,8},{8,0},{1,9},{9,1},{2,10},{10,2},{3,11},{11,3},{4,12},{12,4},... | collective-permute-start | bytes 786440 | tf_op jit(solution)/shard_map/ppermute | solution.py:115
  146.0 13.7 %copy-start.1 = (f32[128,1024]{1,0:T(8,128)S(1)}, f32[128,1024]{1,0:T(8,128)}, u32[]{:S(2)}) copy-start(f32[128,1024]{1,0:T(8,128)} %param.2) | copy-start | bytes 1572868

commit v2 on v1

v2 whole, which is shorter than its diff:
```python
import math

import jax
import jax.numpy as jnp
from jax import lax
from jax.experimental import pallas as pl
from jax.experimental.pallas import tpu as pltpu
from jax.sharding import Mesh
from jax.sharding import PartitionSpec as P

HIGHEST = lax.Precision.HIGHEST
SPLIT = 98304.0


def invert_small(block):
    size = block.shape[0]
    entry = [[jnp.broadcast_to(block[i : i + 1, j : j + 1], (8, 128)) for j in range(i + 1)] for i in range(size)]
    recip = []
    lower = [[None] * size for _ in range(size)]
    for j in range(size):
        r = lax.rsqrt(entry[j][j])
        recip.append(r)
        for i in range(j + 1, size):
            lower[i][j] = entry[i][j] * r
        for i in range(j + 1, size):
            for m in range(j + 1, i + 1):
                entry[i][m] = entry[i][m] - lower[i][j] * lower[m][j]
    inv = [[None] * size for _ in range(size)]
    for j in range(size):
        inv[j][j] = recip[j]
        for i in range(j + 1, size):
            total = lower[i][j] * inv[j][j]
            for m in range(j + 1, i):
                total = total + lower[i][m] * inv[m][j]
            inv[i][j] = -(recip[i] * total)
    return inv


def wide(x, width):
    return jnp.concatenate([x] * (width // 128), axis=1)


def eliminate(m_ref):
    width = 384
    sub = lax.broadcasted_iota(jnp.int32, (8, 128), 0)
    zero = jnp.zeros((8, 128), jnp.float32)
    for half in range(2):
        base = 128 * half
        cols = slice(base, base + width)
        for p in range(16):
            k = base + 8 * p
            rows = m_ref[k : k + 8, cols]
            inv = invert_small(rows[:, 8 * p : 8 * p + 8])
            panel = None
            for j in range(8):
                coef = zero
                for i in range(j, 8):
                    coef = jnp.where(sub == i, inv[i][j], coef)
                term = wide(coef, width) * jnp.broadcast_to(rows[j : j + 1, :], (8, width))
                panel = term if panel is None else panel + term
            m_ref[k : k + 8, cols] = panel
            if p == 15:
                continue
            solved = None
            for j in range(8):
                coef = zero
                for m in range(j + 1):
                    coef = jnp.where(sub == m, inv[j][m], coef)
                term = wide(coef, width) * jnp.broadcast_to(panel[j : j + 1, :], (8, width))
                solved = term if solved is None else solved + term
            spread_rows = [jnp.broadcast_to(solved[m : m + 1, :], (8, width)) for m in range(8)]
            for rb in range(p + 1, 16):
                i = base + 8 * rb
                left = m_ref[i : i + 8, k : k + 8]
                acc = m_ref[i : i + 8, cols]
                for m in range(8):
                    acc = acc - wide(jnp.broadcast_to(left[:, m : m + 1], (8, 128)), width) * spread_rows[m]
                m_ref[i : i + 8, cols] = acc
        if half == 0:
            top = m_ref[0:128, 128:384]
            left = m_ref[0:128, 128:256].T
            m_ref[128:256, 128:384] = m_ref[128:256, 128:384] - jnp.dot(
                left, top, preferred_element_type=jnp.float32, precision=HIGHEST
            )


def two_sum(a, b):
    t = a + b
    z = t - a
    return t, (a - (t - z)) + (b - z)


def add_pairs(a_hi, a_lo, b_hi, b_lo):
    hi, err = two_sum(a_hi, b_hi)
    return hi, err + (a_lo + b_lo)


def slices_of(x, bound, count, tail=None):
    out = []
    for a in range(count):
        step = bound * (SPLIT * 2.0 ** (-8 * a))
        part = (x + step) - step
        x = x - part
        out.append(part)
        if tail is not None and a == 2:
            x = x + tail
    return out


def sum_products(lefts, rights, contract):
    order = sorted((a + b, a, b) for a in range(len(lefts)) for b in range(len(rights)))
    hi = lo = None
    for rank, a, b in order:
        prod = lax.dot_general(lefts[a], rights[b], (contract, ((), ())), preferred_element_type=jnp.float32)
        if hi is None:
            hi, lo = prod, jnp.zeros_like(prod)
        elif rank <= 2:
            hi, err = two_sum(hi, prod)
            lo = lo + err
        else:
            lo = lo + prod
    return two_sum(hi, lo)


def gram_kernel(s_ref, o_ref):
    x = s_ref[...]
    bound = jnp.max(jnp.abs(x), axis=0, keepdims=True)
    parts = slices_of(x, bound, 3)
    rights = [part.astype(jnp.bfloat16) for part in parts]
    lefts = [part.T.astype(jnp.bfloat16) for part in parts]
    for c in range(2):
        pair = sum_products([left[128 * c : 128 * c + 128] for left in lefts], rights, ((1,), (0,)))
        for rb in range(16):
            for h in range(2):
                for w in range(2):
                    o_ref[32 * c + 2 * rb + h, w] = pair[w][8 * rb : 8 * rb + 8, 128 * h : 128 * h + 128]


def chip_kernel(a_ref, b_ref, o_ref):
    o_ref[:, 0], o_ref[:, 1] = add_pairs(a_ref[:, 0], a_ref[:, 1], b_ref[:, 0], b_ref[:, 1])


def total_kernel(a_ref, o_ref):
    pairs = [(a_ref[i, 0], a_ref[i, 1]) for i in range(64)]
    while len(pairs) > 1:
        pairs = [add_pairs(*pairs[i], *pairs[i + 1]) for i in range(0, len(pairs), 2)]
    hi, lo = two_sum(*pairs[0])
    for i in range(64):
        o_ref[i, 0] = hi
        o_ref[i, 1] = lo


def power_below(x):
    return ((x + x * 8.429369702178807e-08) - x) * 8388608.0


def factor_kernel(v_ref, w_ref, m_ref, hi_ref, lo_ref, g_ref, f_ref, t_ref):
    n = 256
    for rb in range(32):
        for h in range(2):
            hi_ref[8 * rb : 8 * rb + 8, 128 * h : 128 * h + 128] = v_ref[2 * rb + h, 0]
            lo_ref[8 * rb : 8 * rb + 8, 128 * h : 128 * h + 128] = v_ref[2 * rb + h, 1]
    diagonal = lax.broadcasted_iota(jnp.int32, (n, n), 0) == lax.broadcasted_iota(jnp.int32, (n, n), 1)
    identity = jnp.where(diagonal, 1.0, 0.0).astype(jnp.float32)
    on_diagonal = jnp.where(diagonal, hi_ref[...], 0.0)
    scale_row = power_below(lax.rsqrt(jnp.sum(on_diagonal, axis=0, keepdims=True)))
    scale_col = power_below(lax.rsqrt(jnp.sum(on_diagonal, axis=1, keepdims=True)))
    hi = hi_ref[...] * scale_row * scale_col
    lo = lo_ref[...] * scale_row * scale_col
    for a, part in enumerate(slices_of(hi, 1.0, 5, lo)):
        g_ref[a] = part.astype(jnp.bfloat16)
    m_ref[:, :n] = hi
    m_ref[:, n:] = identity
    eliminate(m_ref)
    first = m_ref[:, n:]
    parts = slices_of(first, jnp.max(jnp.abs(first), axis=1, keepdims=True), 3)
    for a, part in enumerate(parts):
        f_ref[a] = part.astype(jnp.bfloat16)
    hi_ref[...] = parts[0] + (parts[1] + parts[2])
    for c in range(2):
        rows = slice(128 * c, 128 * c + 128)
        hi, lo = sum_products([f_ref[a, rows] for a in range(3)], [g_ref[a] for a in range(5)], ((1,), (0,)))
        for a, part in enumerate(slices_of(hi, 1.0, 5, lo)):
            t_ref[a, rows] = part.astype(jnp.bfloat16)
    for c in range(2):
        rows = slice(128 * c, 128 * c + 128)
        hi, lo = sum_products([t_ref[a, rows] for a in range(5)], [f_ref[a] for a in range(3)], ((1,), (1,)))
        m_ref[rows, :n] = hi
    m_ref[:, n:] = identity
    eliminate(m_ref)
    w_ref[...] = scale_row * jnp.dot(
        m_ref[:, n:], hi_ref[...], preferred_element_type=jnp.float32, precision=HIGHEST
    )


def call(kernel, shape, *args, scratch=()):
    vmem = pl.BlockSpec(memory_space=pltpu.VMEM)
    return pl.pallas_call(
        kernel,
        out_shape=jax.ShapeDtypeStruct(shape, jnp.float32),
        in_specs=[vmem] * len(args),
        out_specs=vmem,
        scratch_shapes=scratch,
        name=kernel.__name__,
    )(*args)


PAIRS = (64, 2, 8, 128)


def inverse_factor(pairs):
    return call(
        factor_kernel,
        (256, 256),
        pairs,
        scratch=[
            pltpu.VMEM((256, 512), jnp.float32),
            pltpu.VMEM((256, 256), jnp.float32),
            pltpu.VMEM((256, 256), jnp.float32),
            pltpu.VMEM((5, 256, 256), jnp.bfloat16),
            pltpu.VMEM((3, 256, 256), jnp.bfloat16),
            pltpu.VMEM((5, 256, 256), jnp.bfloat16),
        ],
    )


def dot(left, right, contract):
    return lax.dot_general(
        left, right, ((contract[:1], contract[1:]), ((), ())), precision=HIGHEST, preferred_element_type=jnp.float32
    )


def exchange(parts, axes):
    return lax.all_to_all(parts, axes, 0, 0, tiled=True)


def scatter_sum(parts, axes):
    return jnp.sum(exchange(parts, axes), axis=0)


def spread(part, axes, count):
    return exchange(jnp.broadcast_to(part[None], (count, *part.shape)), axes)


def on_device(deposit_maps, test_matrix):
    partial_sketch = dot(deposit_maps, test_matrix, (1, 0))
    part = scatter_sum(partial_sketch.reshape(8, 16, 256), "col")
    sketch = spread(part, "col", 8).reshape(128, 256)
    mine = call(gram_kernel, PAIRS, sketch)
    other = lax.ppermute(mine, "core", [(0, 1), (1, 0)])
    chip = call(chip_kernel, PAIRS, mine, other)
    total = call(total_kernel, PAIRS, exchange(chip, ("z", "x")))
    inverse = inverse_factor(exchange(total, ("z", "x")))
    orthonormal = dot(sketch, inverse, (1, 1))
    total_rows = orthonormal.shape[0] * 128
    scaled_basis = orthonormal * math.sqrt(total_rows)
    halves = dot(orthonormal, deposit_maps, (0, 0)).reshape(64, 2, 2, 1024).transpose(1, 0, 2, 3)
    projected = scatter_sum(scatter_sum(halves, "core"), ("z", "x"))
    return (scaled_basis, projected)


def solution(mesh):
    chips = Mesh(mesh.devices.reshape(8, 8, 2, 8), ("z", "x", "core", "col"))
    rows = ("z", "x", "core")
    return jax.shard_map(
        on_device,
        mesh=chips,
        in_specs=(P(rows, "col"), P("col", None)),
        out_specs=(P(rows, None), P(rows, "col")),
        check_vma=False,
    )
```

time: 202 us -> 173 us (0.86)
  blocking collectives: 145 us -> 113 us
  Pallas kernels: 23.4 us -> 33.2 us
  starting transfers between devices: 18.2 us -> 12.9 us
  matrix products: 6.88 us -> 4.77 us
    all_to_all x7 -> x6, blocking collectives: 145 us -> 113 us  [exchange(): return lax.all_to_all(parts, axes, 0, 0, tiled=True)]
    pallas_call x2 -> x4, Pallas kernels: 23.4 us -> 33.2 us  [call(): pl.pallas_call(kernel, out_shape=jax.ShapeDtypeStruct(shape, jnp.float32)...]
    ppermute x2 -> x1, starting transfers between devices: 18.2 us -> 12.9 us  [on_device(): other = lax.ppermute(mine, 'core', [(0, 1), (1, 0)])]
    dot_general x6 -> x3, matrix products: 6.88 us -> 4.77 us  [dot(): lax.dot_general(left, right, ((contract[:1], contract[1:]), ((), ())), pr...]
  transfers between devices with their start and end apart: 2 -> 1, of which waited for: 2 -> 1; matrix products, arithmetic and copies ran while one was open for 0% -> 0% of each run, Pallas kernels for 0% -> 0%
where the time goes in v2:
time: 173 us; the launch traced here: 171 us
  blocking collectives  113 us (65%)
  Pallas kernels  33.2 us (19%)
  starting transfers between devices  12.9 us (7%)
  matrix products  4.77 us (3%)
  local copies, waits for them, and re-layouts  2.75 us (2%)
  other arithmetic  1.75 us (1%)
  waiting for transfers between devices  1.73 us (1%)
    all_to_all x6, blocking collectives, exchange(): return lax.all_to_all(parts, axes, 0, 0, tiled=True)  113 us
    pallas_call x4, Pallas kernels, call(): pl.pallas_call(kernel, out_shape=jax.ShapeDtypeStruct(shape, jnp.float32)...  33.2 us
    ppermute x1, starting transfers between devices, on_device(): other = lax.ppermute(mine, 'core', [(0, 1), (1, 0)])  12.9 us
    dot_general x3, matrix products, dot(): lax.dot_general(left, right, ((contract[:1], contract[1:]), ((), ())), pr...  4.77 us
  transfers between devices with their start and end apart: 1, of which 1 were waited for; matrix products, arithmetic and copies ran while one was open for 0% of the time, Pallas kernels for 0%

profile of v2, /device:TPU:1, one launch (start us, length us, event | category | flops | bytes accessed | tf_op | source)
XLA Modules:
  0.0 170.8 jit_solution(7198563333173340726)
XLA Ops:
  0.6 0.0 copy-start
  0.6 1.2 copy-done
  1.9 1.7 fusion
  3.5 15.8 %all_to_all.30 = f32[8,16,256]{2,1,0:T(8,128)S(1)} all-to-all(f32[8,16,256]{2,1,0:T(8,128)S(1)} %bitcast.14), channel_id=1, replica_groups=mesh['z'=8,'x'=8,'core'=2,'col'=8] {'col'}, dimensions={0} | all-to-all | bytes 262144 | tf_op jit(solution)/shard_map/all_to_all | solution.py:234
  19.4 11.0 %all_to_all.31 = f32[8,16,256]{2,1,0:T(8,128)} all-to-all(f32[8,16,256]{2,1,0:T(8,128)S(1)} %broadcast_in_dim.2), channel_id=1, replica_groups=mesh['z'=8,'x'=8,'core'=2,'col'=8] {'col'}, dimensions={0} | all-to-all | bytes 262144 | tf_op jit(solution)/shard_map/all_to_all | solution.py:234
  30.4 2.4 %gram_kernel.1.a_ref = f32[64,2,8,128]{3,2,1,0:T(8,128)} custom-call(f32[128,256]{1,0:T(8,128)} %bitcast.12), custom_call_target="tpu_custom_call" | custom-call | tf_op jit(solution)/shard_map/gram_kernel/pallas_call | solution.py:198
  32.8 12.9 %collective-permute-start = (f32[64,2,8,128]{3,2,1,0:T(8,128)}, f32[64,2,8,128]{3,2,1,0:T(8,128)S(1)}, u32[]{:S(2)}, u32[]{:S(2)}) collective-permute-start(f32[64,2,8,128]{3,2,1,0:T(8,128)} %gram_kernel.1.a_ref), channel_id=1, source_target_pairs={{0,8},{8,0},{1,9},{9,1},{2,10},{10,2},{3,11},{11,3},{4,12},{12,4},... | collective-permute-start | bytes 1572872 | tf_op jit(solution)/shard_map/ppermute | solution.py:250
  45.7 1.7 %collective-permute-done.b_ref = f32[64,2,8,128]{3,2,1,0:T(8,128)S(1)} collective-permute-done((f32[64,2,8,128]{3,2,1,0:T(8,128)}, f32[64,2,8,128]{3,2,1,0:T(8,128)S(1)}, u32[]{:S(2)}, u32[]{:S(2)}) %collective-permute-start) | collective-permute-done | bytes 524320 | tf_op jit(solution)/shard_map/ppermute | solution.py:250
  47.4 0.0 copy-start.3
  47.4 0.8 copy-done.3
  48.2 2.1 %chip_kernel.1 = f32[64,2,8,128]{3,2,1,0:T(8,128)} custom-call(f32[64,2,8,128]{3,2,1,0:T(8,128)} %gram_kernel.1.a_ref, f32[64,2,8,128]{3,2,1,0:T(8,128)} %copy-done.3), custom_call_target="tpu_custom_call" | custom-call | tf_op jit(solution)/shard_map/chip_kernel/pallas_call | solution.py:198
  50.3 32.4 %all_to_all.32.a_ref = f32[64,2,8,128]{3,2,1,0:T(8,128)} all-to-all(f32[64,2,8,128]{3,2,1,0:T(8,128)} %chip_kernel.1), channel_id=1, replica_groups=mesh['z'=8,'x'=8,'core'=2,'col'=8] {'z','x'}, dimensions={0} | all-to-all | bytes 1048576 | tf_op jit(solution)/shard_map/all_to_all | solution.py:234
  82.7 1.9 %total_kernel.1 = f32[64,2,8,128]{3,2,1,0:T(8,128)} custom-call(f32[64,2,8,128]{3,2,1,0:T(8,128)} %all_to_all.32.a_ref), custom_call_target="tpu_custom_call" | custom-call | tf_op jit(solution)/shard_map/total_kernel/pallas_call | solution.py:198
  84.7 23.4 %all_to_all.33.v_ref = f32[64,2,8,128]{3,2,1,0:T(8,128)} all-to-all(f32[64,2,8,128]{3,2,1,0:T(8,128)} %total_kernel.1), channel_id=1, replica_groups=mesh['z'=8,'x'=8,'core'=2,'col'=8] {'z','x'}, dimensions={0} | all-to-all | bytes 1048576 | tf_op jit(solution)/shard_map/all_to_all | solution.py:234
  108.1 0.0 copy-start.2
  108.1 26.8 %factor_kernel.1 = f32[256,256]{1,0:T(8,128)} custom-call(f32[64,2,8,128]{3,2,1,0:T(8,128)} %all_to_all.33.v_ref), custom_call_target="tpu_custom_call" | custom-call | tf_op jit(solution)/shard_map/factor_kernel/pallas_call | solution.py:198
  134.9 0.0 copy-done.2
  134.9 0.0 copy-start.1
  134.9 2.1 %broadcast_multiply_fusion = (f32[128,256]{1,0:T(8,128)}, f32[128,256]{1,0:T(8,128)S(1)}) fusion(f32[128,256]{1,0:T(8,128)S(1)} %bitcast.13, f32[256,256]{1,0:T(8,128)} %factor_kernel.1), kind=kOutput, calls=%fused_computation.1 | convolution fusion | flops 100696064 | bytes 655360 | tf_op jit(solution)/shard_map/dot_general | solution.py:228
  137.0 0.0 copy-done.1
  137.0 1.0 fusion.1
  138.0 0.6 reshape.16
  138.7 0.1 copy.10
  138.7 8.1 %all_to_all.34 = f32[2,64,2,1024]{3,2,1,0:T(2,128)S(1)} all-to-all(f32[2,64,2,1024]{3,2,1,0:T(2,128)S(1)} %bitcast.11), channel_id=1, replica_groups=mesh['z'=8,'x'=8,'core'=2,'col'=8] {'core'}, dimensions={0} | all-to-all | bytes 2097152 | tf_op jit(solution)/shard_map/all_to_all | solution.py:234
  146.8 0.9 reduce_sum.28
  147.8 22.2 %all_to_all.35 = f32[64,2,1024]{2,1,0:T(2,128)S(1)} all-to-all(f32[64,2,1024]{2,1,0:T(2,128)S(1)} %reduce_sum.28), channel_id=1, replica_groups=mesh['z'=8,'x'=8,'core'=2,'col'=8] {'z','x'}, dimensions={0} | all-to-all | bytes 1048576 | tf_op jit(solution)/shard_map/all_to_all | solution.py:234
  170.0 0.8 reduce_sum.29
  (2 shorter events, 0.0 us)
Async XLA Ops:
  0.6 1.2 copy-start
  32.8 14.6 %collective-permute-start = (f32[64,2,8,128]{3,2,1,0:T(8,128)}, f32[64,2,8,128]{3,2,1,0:T(8,128)S(1)}, u32[]{:S(2)}, u32[]{:S(2)}) collective-permute-start(f32[64,2,8,128]{3,2,1,0:T(8,128)} %gram_kernel.1.a_ref), channel_id=1, source_target_pairs={{0,8},{8,0},{1,9},{9,1},{2,10},{10,2},{3,11},{11,3},{4,12},{12,4},... | collective-permute-start | bytes 1572872 | tf_op jit(solution)/shard_map/ppermute | solution.py:250
  47.4 0.8 copy-start.3
  108.1 26.8 %copy-start.2 = (f32[8,16,256]{2,1,0:T(8,128)S(1)}, f32[8,16,256]{2,1,0:T(8,128)}, u32[]{:S(2)}) copy-start(f32[8,16,256]{2,1,0:T(8,128)} %all_to_all.31) | copy-start | bytes 393220
  134.9 2.1 %copy-start.1 = (f32[128,1024]{1,0:T(8,128)S(1)}, f32[128,1024]{1,0:T(8,128)}, u32[]{:S(2)}) copy-start(f32[128,1024]{1,0:T(8,128)} %param.2) | copy-start | bytes 1572868

commit v3 on v2

--- a/solution.py
+++ b/solution.py
@@ -90,9 +90,12 @@
     return t, (a - (t - z)) + (b - z)
 
 
-def add_pairs(a_hi, a_lo, b_hi, b_lo):
-    hi, err = two_sum(a_hi, b_hi)
-    return hi, err + (a_lo + b_lo)
+def top_half(shape):
+    return lax.broadcasted_iota(jnp.int32, shape, len(shape) - 2) % 8 < 4
+
+
+def swap(x):
+    return pltpu.roll(x, 4, x.ndim - 2)
 
 
 def slices_of(x, bound, count, tail=None):
@@ -107,10 +110,12 @@
     return out
 
 
-def sum_products(lefts, rights, contract):
+def sum_products(lefts, rights, contract, last_rank=8):
     order = sorted((a + b, a, b) for a in range(len(lefts)) for b in range(len(rights)))
     hi = lo = None
     for rank, a, b in order:
+        if rank > last_rank:
+            break
         prod = lax.dot_general(lefts[a], rights[b], (contract, ((), ())), preferred_element_type=jnp.float32)
         if hi is None:
             hi, lo = prod, jnp.zeros_like(prod)
@@ -129,37 +134,48 @@
     rights = [part.astype(jnp.bfloat16) for part in parts]
     lefts = [part.T.astype(jnp.bfloat16) for part in parts]
     for c in range(2):
-        pair = sum_products([left[128 * c : 128 * c + 128] for left in lefts], rights, ((1,), (0,)))
-        for rb in range(16):
-            for h in range(2):
-                for w in range(2):
-                    o_ref[32 * c + 2 * rb + h, w] = pair[w][8 * rb : 8 * rb + 8, 128 * h : 128 * h + 128]
-
-
-def chip_kernel(a_ref, b_ref, o_ref):
-    o_ref[:, 0], o_ref[:, 1] = add_pairs(a_ref[:, 0], a_ref[:, 1], b_ref[:, 0], b_ref[:, 1])
+        hi, lo = sum_products([left[128 * c : 128 * c + 128] for left in lefts], rights, ((1,), (0,)))
+        for tile in range(32):
+            block = (slice(8 * (tile // 2), 8 * (tile // 2) + 8), slice(128 * (tile % 2), 128 * (tile % 2) + 128))
+            o_ref[c, 2 * tile] = jnp.where(top_half((8, 128)), hi[block], swap(lo[block]))
+            o_ref[c, 2 * tile + 1] = jnp.where(top_half((8, 128)), swap(hi[block]), lo[block])
+
+
+def chip_kernel(a_ref, o_ref):
+    total, err = two_sum(a_ref[0], a_ref[1])
+    o_ref[...] = total + jnp.where(top_half(err.shape), 0.0, swap(err))
 
 
 def total_kernel(a_ref, o_ref):
-    pairs = [(a_ref[i, 0], a_ref[i, 1]) for i in range(64)]
-    while len(pairs) > 1:
-        pairs = [add_pairs(*pairs[i], *pairs[i + 1]) for i in range(0, len(pairs), 2)]
-    hi, lo = two_sum(*pairs[0])
+    terms = [(a_ref[i], None) for i in range(64)]
+    while len(terms) > 1:
+        merged = []
+        for (x, x_err), (y, y_err) in zip(terms[::2], terms[1::2]):
+            total, err = two_sum(x, y)
+            merged.append((total, err if x_err is None else err + (x_err + y_err)))
+        terms = merged
+    total, err = terms[0]
+    total = total + jnp.where(top_half((8, 128)), 0.0, swap(err))
     for i in range(64):
-        o_ref[i, 0] = hi
-        o_ref[i, 1] = lo
+        o_ref[i] = total
 
 
 def power_below(x):
     return ((x + x * 8.429369702178807e-08) - x) * 8388608.0
 
 
-def factor_kernel(v_ref, w_ref, m_ref, hi_ref, lo_ref, g_ref, f_ref, t_ref):
+def factor_kernel(core_ref, mine_ref, other_ref, w_ref, m_ref, hi_ref, lo_ref, g_ref, f_ref, t_ref):
     n = 256
-    for rb in range(32):
-        for h in range(2):
-            hi_ref[8 * rb : 8 * rb + 8, 128 * h : 128 * h + 128] = v_ref[2 * rb + h, 0]
-            lo_ref[8 * rb : 8 * rb + 8, 128 * h : 128 * h + 128] = v_ref[2 * rb + h, 1]
+    for half_ref, base in ((mine_ref, 128 * core_ref[0]), (other_ref, 128 * (1 - core_ref[0]))):
+        for tile in range(32):
+            first, second = half_ref[2 * tile], half_ref[2 * tile + 1]
+            rows = pl.ds(pl.multiple_of(base + 8 * (tile // 2), 8), 8)
+            cols = slice(128 * (tile % 2), 128 * (tile % 2) + 128)
+            hi, lo = two_sum(
+                jnp.where(top_half((8, 128)), first, swap(second)), jnp.where(top_half((8, 128)), swap(first), second)
+            )
+            hi_ref[rows, cols] = hi
+            lo_ref[rows, cols] = lo
     diagonal = lax.broadcasted_iota(jnp.int32, (n, n), 0) == lax.broadcasted_iota(jnp.int32, (n, n), 1)
     identity = jnp.where(diagonal, 1.0, 0.0).astype(jnp.float32)
     on_diagonal = jnp.where(diagonal, hi_ref[...], 0.0)
@@ -184,7 +200,7 @@
             t_ref[a, rows] = part.astype(jnp.bfloat16)
     for c in range(2):
         rows = slice(128 * c, 128 * c + 128)
-        hi, lo = sum_products([t_ref[a, rows] for a in range(5)], [f_ref[a] for a in range(3)], ((1,), (1,)))
+        hi, lo = sum_products([t_ref[a, rows] for a in range(5)], [f_ref[a] for a in range(3)], ((1,), (1,)), 4)
         m_ref[rows, :n] = hi
     m_ref[:, n:] = identity
     eliminate(m_ref)
@@ -193,26 +209,32 @@
     )
 
 
-def call(kernel, shape, *args, scratch=()):
+def call(kernel, shape, *args, scalar=None, scratch=()):
     vmem = pl.BlockSpec(memory_space=pltpu.VMEM)
+    specs = [vmem] * len(args)
+    if scalar is not None:
+        args = (scalar, *args)
+        specs = [pl.BlockSpec(memory_space=pltpu.SMEM), *specs]
     return pl.pallas_call(
         kernel,
         out_shape=jax.ShapeDtypeStruct(shape, jnp.float32),
-        in_specs=[vmem] * len(args),
+        in_specs=specs,
         out_specs=vmem,
         scratch_shapes=scratch,
         name=kernel.__name__,
     )(*args)
 
 
-PAIRS = (64, 2, 8, 128)
-
-
-def inverse_factor(pairs):
+HALF = (64, 8, 128)
+
+
+def inverse_factor(core, mine, other):
     return call(
         factor_kernel,
         (256, 256),
-        pairs,
+        mine,
+        other,
+        scalar=core,
         scratch=[
             pltpu.VMEM((256, 512), jnp.float32),
             pltpu.VMEM((256, 256), jnp.float32),
@@ -246,11 +268,11 @@
     partial_sketch = dot(deposit_maps, test_matrix, (1, 0))
     part = scatter_sum(partial_sketch.reshape(8, 16, 256), "col")
     sketch = spread(part, "col", 8).reshape(128, 256)
-    mine = call(gram_kernel, PAIRS, sketch)
+    pairs = exchange(call(gram_kernel, (2, *HALF), sketch), "core")
+    chip = call(chip_kernel, HALF, pairs)
+    mine = exchange(call(total_kernel, HALF, exchange(chip, ("z", "x"))), ("z", "x"))
     other = lax.ppermute(mine, "core", [(0, 1), (1, 0)])
-    chip = call(chip_kernel, PAIRS, mine, other)
-    total = call(total_kernel, PAIRS, exchange(chip, ("z", "x")))
-    inverse = inverse_factor(exchange(total, ("z", "x")))
+    inverse = inverse_factor(lax.axis_index("core").reshape(1), mine, other)
     orthonormal = dot(sketch, inverse, (1, 1))
     total_rows = orthonormal.shape[0] * 128
     scaled_basis = orthonormal * math.sqrt(total_rows)

time: 173 us -> 166 us (0.960)
  starting transfers between devices: 12.9 us -> 5.49 us
  blocking collectives: 113 us -> 116 us
    ppermute x1, starting transfers between devices: 12.9 us -> 5.49 us  [on_device(): other = lax.ppermute(mine, 'core', [(0, 1), (1, 0)])]
    all_to_all x6 -> x7, blocking collectives: 113 us -> 116 us  [exchange(): return lax.all_to_all(parts, axes, 0, 0, tiled=True)]
where the time goes in v3:
time: 166 us; the launch traced here: 165 us
  blocking collectives  116 us (70%)
  Pallas kernels  32.7 us (20%)
  starting transfers between devices  5.49 us (3%)
  matrix products  4.77 us (3%)
  local copies, waits for them, and re-layouts  2.63 us (2%)
  other arithmetic  1.75 us (1%)
    all_to_all x7, blocking collectives, exchange(): return lax.all_to_all(parts, axes, 0, 0, tiled=True)  116 us
    pallas_call x4, Pallas kernels, call(): pl.pallas_call(kernel, out_shape=jax.ShapeDtypeStruct(shape, jnp.float32)...  32.7 us
    ppermute x1, starting transfers between devices, on_device(): other = lax.ppermute(mine, 'core', [(0, 1), (1, 0)])  5.49 us
    dot_general x3, matrix products, dot(): lax.dot_general(left, right, ((contract[:1], contract[1:]), ((), ())), pr...  4.77 us
  transfers between devices with their start and end apart: 1, of which 1 were waited for; matrix products, arithmetic and copies ran while one was open for 0% of the time, Pallas kernels for 0%

profile of v3, /device:TPU:1, one launch (start us, length us, event | category | flops | bytes accessed | tf_op | source)
XLA Modules:
  0.0 164.5 jit_solution(12680684334096657729)
XLA Ops:
  0.6 0.0 copy-start
  0.6 1.2 copy-done
  1.9 1.7 %fusion = f32[128,256]{1,0:T(8,128)S(1)} fusion(f32[128,1024]{1,0:T(8,128)} %param.2, f32[1024,256]{1,0:T(8,128)S(1)} %copy-done), kind=kOutput, calls=%fused_computation.2 | convolution fusion | flops 402653184 | bytes 1703936 | tf_op jit(solution)/shard_map/dot_general | solution.py:250
  3.5 15.8 %all_to_all.35 = f32[8,16,256]{2,1,0:T(8,128)S(1)} all-to-all(f32[8,16,256]{2,1,0:T(8,128)S(1)} %bitcast.15), channel_id=1, replica_groups=mesh['z'=8,'x'=8,'core'=2,'col'=8] {'col'}, dimensions={0} | all-to-all | bytes 262144 | tf_op jit(solution)/shard_map/all_to_all | solution.py:256
  19.4 11.0 %all_to_all.36 = f32[8,16,256]{2,1,0:T(8,128)} all-to-all(f32[8,16,256]{2,1,0:T(8,128)S(1)} %broadcast_in_dim.2), channel_id=1, replica_groups=mesh['z'=8,'x'=8,'core'=2,'col'=8] {'col'}, dimensions={0} | all-to-all | bytes 262144 | tf_op jit(solution)/shard_map/all_to_all | solution.py:256
  30.4 2.4 %gram_kernel.1 = f32[2,64,8,128]{3,2,1,0:T(8,128)} custom-call(f32[128,256]{1,0:T(8,128)} %bitcast.13), custom_call_target="tpu_custom_call" | custom-call | tf_op jit(solution)/shard_map/gram_kernel/pallas_call | solution.py:218
  32.8 16.7 %all_to_all.37.a_ref = f32[2,64,8,128]{3,2,1,0:T(8,128)} all-to-all(f32[2,64,8,128]{3,2,1,0:T(8,128)} %gram_kernel.1), channel_id=1, replica_groups=mesh['z'=8,'x'=8,'core'=2,'col'=8] {'core'}, dimensions={0} | all-to-all | bytes 1048576 | tf_op jit(solution)/shard_map/all_to_all | solution.py:256
  49.5 1.8 %chip_kernel.1 = f32[64,8,128]{2,1,0:T(8,128)} custom-call(f32[2,64,8,128]{3,2,1,0:T(8,128)} %all_to_all.37.a_ref), custom_call_target="tpu_custom_call" | custom-call | tf_op jit(solution)/shard_map/chip_kernel/pallas_call | solution.py:218
  51.3 27.9 %all_to_all.38.a_ref = f32[64,8,128]{2,1,0:T(8,128)} all-to-all(f32[64,8,128]{2,1,0:T(8,128)} %chip_kernel.1), channel_id=1, replica_groups=mesh['z'=8,'x'=8,'core'=2,'col'=8] {'z','x'}, dimensions={0} | all-to-all | bytes 524288 | tf_op jit(solution)/shard_map/all_to_all | solution.py:256
  79.2 1.7 %total_kernel.1 = f32[64,8,128]{2,1,0:T(8,128)} custom-call(f32[64,8,128]{2,1,0:T(8,128)} %all_to_all.38.a_ref), custom_call_target="tpu_custom_call" | custom-call | tf_op jit(solution)/shard_map/total_kernel/pallas_call | solution.py:218
  81.0 17.9 %all_to_all.39.mine_ref = f32[64,8,128]{2,1,0:T(8,128)S(1)} all-to-all(f32[64,8,128]{2,1,0:T(8,128)} %total_kernel.1), channel_id=1, replica_groups=mesh['z'=8,'x'=8,'core'=2,'col'=8] {'z','x'}, dimensions={0} | all-to-all | bytes 524288 | tf_op jit(solution)/shard_map/all_to_all | solution.py:256
  98.9 0.0 copy-start.3
  98.9 5.5 %collective-permute-start = (f32[64,8,128]{2,1,0:T(8,128)S(1)}, f32[64,8,128]{2,1,0:T(8,128)S(1)}, u32[]{:S(2)}, u32[]{:S(2)}) collective-permute-start(f32[64,8,128]{2,1,0:T(8,128)S(1)} %all_to_all.39.mine_ref), channel_id=1, source_target_pairs={{0,8},{8,0},{1,9},{9,1},{2,10},{10,2},{3,11},{11,3},{4,12},{12,4},... | collective-permute-start | bytes 786440 | tf_op jit(solution)/shard_map/ppermute | solution.py:274
  104.4 1.0 collective-permute-done.other_ref
  105.4 0.0 copy-start.4
  105.4 0.0 copy-done.3
  105.4 0.7 copy-done.4
  106.1 0.0 copy-start.2
  106.1 26.7 %factor_kernel.1 = f32[256,256]{1,0:T(8,128)} custom-call(s32[1]{0:T(128)} %bitcast.2.core_ref, f32[64,8,128]{2,1,0:T(8,128)} %copy-done.3, f32[64,8,128]{2,1,0:T(8,128)} %copy-done.4), custom_call_target="tpu_custom_call" | custom-call | tf_op jit(solution)/shard_map/factor_kernel/pallas_call | solution.py:218
  132.8 0.0 copy-done.2
  132.8 0.0 copy-start.1
  132.8 2.1 %broadcast_multiply_fusion = (f32[128,256]{1,0:T(8,128)}, f32[128,256]{1,0:T(8,128)S(1)}) fusion(f32[128,256]{1,0:T(8,128)S(1)} %bitcast.14, f32[256,256]{1,0:T(8,128)} %factor_kernel.1), kind=kOutput, calls=%fused_computation.1 | convolution fusion | flops 100696064 | bytes 655360 | tf_op jit(solution)/shard_map/dot_general | solution.py:250
  134.8 0.0 copy-done.1
  134.8 1.0 fusion.1
  135.9 0.6 reshape.20
  136.5 0.1 copy.10
  136.6 4.6 %all_to_all.40 = f32[2,64,2,1024]{3,2,1,0:T(2,128)S(1)} all-to-all(f32[2,64,2,1024]{3,2,1,0:T(2,128)S(1)} %bitcast.12), channel_id=1, replica_groups=mesh['z'=8,'x'=8,'core'=2,'col'=8] {'core'}, dimensions={0} | all-to-all | bytes 2097152 | tf_op jit(solution)/shard_map/all_to_all | solution.py:256
  141.1 0.9 reduce_sum.28
  142.1 21.6 %all_to_all.41 = f32[64,2,1024]{2,1,0:T(2,128)S(1)} all-to-all(f32[64,2,1024]{2,1,0:T(2,128)S(1)} %reduce_sum.28), channel_id=1, replica_groups=mesh['z'=8,'x'=8,'core'=2,'col'=8] {'z','x'}, dimensions={0} | all-to-all | bytes 1048576 | tf_op jit(solution)/shard_map/all_to_all | solution.py:256
  163.7 0.8 reduce_sum.29
  (2 shorter events, 0.0 us)
Async XLA Ops:
  0.6 1.2 copy-start
  98.9 6.5 %copy-start.3 = (f32[64,8,128]{2,1,0:T(8,128)}, f32[64,8,128]{2,1,0:T(8,128)S(1)}, u32[]{:S(2)}) copy-start(f32[64,8,128]{2,1,0:T(8,128)S(1)} %all_to_all.39.mine_ref) | copy-start | bytes 786436
  98.9 6.5 %collective-permute-start = (f32[64,8,128]{2,1,0:T(8,128)S(1)}, f32[64,8,128]{2,1,0:T(8,128)S(1)}, u32[]{:S(2)}, u32[]{:S(2)}) collective-permute-start(f32[64,8,128]{2,1,0:T(8,128)S(1)} %all_to_all.39.mine_ref), channel_id=1, source_target_pairs={{0,8},{8,0},{1,9},{9,1},{2,10},{10,2},{3,11},{11,3},{4,12},{12,4},... | collective-permute-start | bytes 786440 | tf_op jit(solution)/shard_map/ppermute | solution.py:274
  105.4 0.7 copy-start.4
  106.1 26.7 %copy-start.2 = (f32[8,16,256]{2,1,0:T(8,128)S(1)}, f32[8,16,256]{2,1,0:T(8,128)}, u32[]{:S(2)}) copy-start(f32[8,16,256]{2,1,0:T(8,128)} %all_to_all.36) | copy-start | bytes 393220
  132.8 2.1 %copy-start.1 = (f32[128,1024]{1,0:T(8,128)S(1)}, f32[128,1024]{1,0:T(8,128)}, u32[]{:S(2)}) copy-start(f32[128,1024]{1,0:T(8,128)} %param.2) | copy-start | bytes 1572868

commit v4 on v3

--- a/solution.py
+++ b/solution.py
@@ -127,23 +127,18 @@
     return two_sum(hi, lo)
 
 
-def gram_kernel(s_ref, o_ref):
-    x = s_ref[...]
-    bound = jnp.max(jnp.abs(x), axis=0, keepdims=True)
-    parts = slices_of(x, bound, 3)
-    rights = [part.astype(jnp.bfloat16) for part in parts]
-    lefts = [part.T.astype(jnp.bfloat16) for part in parts]
-    for c in range(2):
-        hi, lo = sum_products([left[128 * c : 128 * c + 128] for left in lefts], rights, ((1,), (0,)))
-        for tile in range(32):
-            block = (slice(8 * (tile // 2), 8 * (tile // 2) + 8), slice(128 * (tile % 2), 128 * (tile % 2) + 128))
-            o_ref[c, 2 * tile] = jnp.where(top_half((8, 128)), hi[block], swap(lo[block]))
-            o_ref[c, 2 * tile + 1] = jnp.where(top_half((8, 128)), swap(hi[block]), lo[block])
-
-
-def chip_kernel(a_ref, o_ref):
-    total, err = two_sum(a_ref[0], a_ref[1])
-    o_ref[...] = total + jnp.where(top_half(err.shape), 0.0, swap(err))
+def gram_kernel(core_ref, s_ref, o_ref):
+    mine = pl.ds(pl.multiple_of(128 * core_ref[0], 128), 128)
+    sides = []
+    for x in (s_ref[:, mine], s_ref[...]):
+        sides.append(slices_of(x, jnp.max(jnp.abs(x), axis=0, keepdims=True), 3))
+    lefts = [part.T.astype(jnp.bfloat16) for part in sides[0]]
+    rights = [part.astype(jnp.bfloat16) for part in sides[1]]
+    hi, lo = sum_products(lefts, rights, ((1,), (0,)))
+    for tile in range(32):
+        block = (slice(8 * (tile // 2), 8 * (tile // 2) + 8), slice(128 * (tile % 2), 128 * (tile % 2) + 128))
+        o_ref[2 * tile] = jnp.where(top_half((8, 128)), hi[block], swap(lo[block]))
+        o_ref[2 * tile + 1] = jnp.where(top_half((8, 128)), swap(hi[block]), lo[block])
 
 
 def total_kernel(a_ref, o_ref):
@@ -267,12 +262,13 @@
 def on_device(deposit_maps, test_matrix):
     partial_sketch = dot(deposit_maps, test_matrix, (1, 0))
     part = scatter_sum(partial_sketch.reshape(8, 16, 256), "col")
-    sketch = spread(part, "col", 8).reshape(128, 256)
-    pairs = exchange(call(gram_kernel, (2, *HALF), sketch), "core")
-    chip = call(chip_kernel, HALF, pairs)
-    mine = exchange(call(total_kernel, HALF, exchange(chip, ("z", "x"))), ("z", "x"))
+    core = lax.axis_index("core").reshape(1)
+    chip = spread(part, ("core", "col"), 16).reshape(256, 256)
+    sketch = lax.dynamic_slice_in_dim(chip, 128 * core[0], 128)
+    pairs = call(gram_kernel, HALF, chip, scalar=core)
+    mine = exchange(call(total_kernel, HALF, exchange(pairs, ("z", "x"))), ("z", "x"))
     other = lax.ppermute(mine, "core", [(0, 1), (1, 0)])
-    inverse = inverse_factor(lax.axis_index("core").reshape(1), mine, other)
+    inverse = inverse_factor(core, mine, other)
     orthonormal = dot(sketch, inverse, (1, 1))
     total_rows = orthonormal.shape[0] * 128
     scaled_basis = orthonormal * math.sqrt(total_rows)

time: 166 us -> 160 us (0.964)
  blocking collectives: 116 us -> 87.8 us
  starting transfers between devices: 5.49 us -> 18.8 us
  waiting for transfers between devices: 0.96 us -> 10.3 us
  Pallas kernels: 32.7 us -> 30.6 us
    all_to_all x7 -> x5, blocking collectives: 116 us -> 87.8 us  [exchange(): return lax.all_to_all(parts, axes, 0, 0, tiled=True)]
    all_to_all x0 -> x1, starting transfers between devices: none -> 13.1 us  [exchange(): return lax.all_to_all(parts, axes, 0, 0, tiled=True)]
    all_to_all x0 -> x1, waiting for transfers between devices: none -> 9.39 us  [exchange(): return lax.all_to_all(parts, axes, 0, 0, tiled=True)]
    pallas_call x4 -> x3, Pallas kernels: 32.7 us -> 30.6 us  [call(): pl.pallas_call(kernel, out_shape=jax.ShapeDtypeStruct(shape, jnp.float32)...]
  transfers between devices with their start and end apart: 1 -> 2, of which waited for: 1 -> 2; matrix products, arithmetic and copies ran while one was open for 0% -> 0% of each run, Pallas kernels for 0% -> 0%
where the time goes in v4:
time: 160 us; the launch traced here: 159 us
  blocking collectives  87.8 us (55%)
  Pallas kernels  30.6 us (19%)
  starting transfers between devices  18.8 us (12%)
  waiting for transfers between devices  10.3 us (6%)
  matrix products  4.78 us (3%)
  local copies, waits for them, and re-layouts  4.03 us (3%)
  other arithmetic  1.75 us (1%)
    all_to_all x5, blocking collectives, exchange(): return lax.all_to_all(parts, axes, 0, 0, tiled=True)  87.8 us
    pallas_call x3, Pallas kernels, call(): pl.pallas_call(kernel, out_shape=jax.ShapeDtypeStruct(shape, jnp.float32)...  30.6 us
    all_to_all x1, starting transfers between devices, exchange(): return lax.all_to_all(parts, axes, 0, 0, tiled=True)  13.1 us
    all_to_all x1, waiting for transfers between devices, exchange(): return lax.all_to_all(parts, axes, 0, 0, tiled=True)  9.39 us
    ppermute x1, starting transfers between devices, on_device(): other = lax.ppermute(mine, 'core', [(0, 1), (1, 0)])  5.68 us
    dot_general x3, matrix products, dot(): lax.dot_general(left, right, ((contract[:1], contract[1:]), ((), ())), pr...  4.78 us
  transfers between devices with their start and end apart: 2, of which 2 were waited for; matrix products, arithmetic and copies ran while one was open for 0% of the time, Pallas kernels for 0%

profile of v4, /device:TPU:1, one launch (start us, length us, event | category | flops | bytes accessed | tf_op | source)
XLA Modules:
  0.0 158.8 jit_solution(7694204462186882041)
XLA Ops:
  0.6 0.0 copy-start
  0.6 1.2 copy-done
  1.9 1.7 %fusion.3 = f32[128,256]{1,0:T(8,128)S(1)} fusion(f32[128,1024]{1,0:T(8,128)} %param.2, f32[1024,256]{1,0:T(8,128)S(1)} %copy-done), kind=kOutput, calls=%fused_computation.5 | convolution fusion | flops 402653184 | bytes 1703936 | tf_op jit(solution)/shard_map/dot_general | solution.py:245
  3.5 15.8 %all_to_all.30 = f32[8,16,256]{2,1,0:T(8,128)S(1)} all-to-all(f32[8,16,256]{2,1,0:T(8,128)S(1)} %bitcast.14), channel_id=1, replica_groups=mesh['z'=8,'x'=8,'core'=2,'col'=8] {'col'}, dimensions={0} | all-to-all | bytes 262144 | tf_op jit(solution)/shard_map/all_to_all | solution.py:251
  19.4 0.7 broadcast_in_dim.2
  20.1 13.1 %all-to-all-start.1 = ((f32[16,16,256]{2,1,0:T(8,128)}), f32[16,16,256]{2,1,0:T(8,128)S(1)}, u32[]{:S(2)}, u32[]{:S(2)}) async-start(f32[16,16,256]{2,1,0:T(8,128)} %broadcast_in_dim.2), calls=%async_computation.1 | async-start | bytes 524288 | tf_op jit(solution)/shard_map/all_to_all | solution.py:251
  33.2 9.4 %all-to-all-done.1 = f32[16,16,256]{2,1,0:T(8,128)S(1)} async-done(((f32[16,16,256]{2,1,0:T(8,128)}), f32[16,16,256]{2,1,0:T(8,128)S(1)}, u32[]{:S(2)}, u32[]{:S(2)}) %all-to-all-start.1) | async-done | bytes 262176 | tf_op jit(solution)/shard_map/all_to_all | solution.py:251
  42.6 0.0 copy-start.2
  42.6 0.7 copy-done.2
  43.3 2.2 %gram_kernel.1 = f32[64,8,128]{2,1,0:T(8,128)} custom-call(s32[1]{0:T(128)} %bitcast.2.core_ref, f32[256,256]{1,0:T(8,128)} %bitcast.12), custom_call_target="tpu_custom_call" | custom-call | tf_op jit(solution)/shard_map/gram_kernel/pallas_call | solution.py:213
  45.5 27.4 %all_to_all.31.a_ref = f32[64,8,128]{2,1,0:T(8,128)} all-to-all(f32[64,8,128]{2,1,0:T(8,128)} %gram_kernel.1), channel_id=1, replica_groups=mesh['z'=8,'x'=8,'core'=2,'col'=8] {'z','x'}, dimensions={0} | all-to-all | bytes 524288 | tf_op jit(solution)/shard_map/all_to_all | solution.py:251
  72.9 1.7 %total_kernel.1 = f32[64,8,128]{2,1,0:T(8,128)} custom-call(f32[64,8,128]{2,1,0:T(8,128)} %all_to_all.31.a_ref), custom_call_target="tpu_custom_call" | custom-call | tf_op jit(solution)/shard_map/total_kernel/pallas_call | solution.py:213
  74.6 18.3 %all_to_all.32.mine_ref = f32[64,8,128]{2,1,0:T(8,128)S(1)} all-to-all(f32[64,8,128]{2,1,0:T(8,128)} %total_kernel.1), channel_id=1, replica_groups=mesh['z'=8,'x'=8,'core'=2,'col'=8] {'z','x'}, dimensions={0} | all-to-all | bytes 524288 | tf_op jit(solution)/shard_map/all_to_all | solution.py:251
  92.9 0.0 copy-start.4
  92.9 5.7 %collective-permute-start = (f32[64,8,128]{2,1,0:T(8,128)S(1)}, f32[64,8,128]{2,1,0:T(8,128)S(1)}, u32[]{:S(2)}, u32[]{:S(2)}) collective-permute-start(f32[64,8,128]{2,1,0:T(8,128)S(1)} %all_to_all.32.mine_ref), channel_id=1, source_target_pairs={{0,8},{8,0},{1,9},{9,1},{2,10},{10,2},{3,11},{11,3},{4,12},{12,4},... | collective-permute-start | bytes 786440 | tf_op jit(solution)/shard_map/ppermute | solution.py:270
  98.6 0.0 copy-start.3
  98.6 0.9 collective-permute-done.other_ref
  99.6 0.0 copy-done.4
  99.6 0.0 copy-start.5
  99.6 0.7 copy-done.5
  100.3 26.7 %factor_kernel.1 = f32[256,256]{1,0:T(8,128)} custom-call(s32[1]{0:T(128)} %bitcast.2.core_ref, f32[64,8,128]{2,1,0:T(8,128)} %copy-done.4, f32[64,8,128]{2,1,0:T(8,128)} %copy-done.5), custom_call_target="tpu_custom_call" | custom-call | tf_op jit(solution)/shard_map/factor_kernel/pallas_call | solution.py:213
  126.9 0.0 copy-done.3
  126.9 0.0 copy-start.1
  126.9 2.1 %broadcast_multiply_fusion = (f32[128,256]{1,0:T(8,128)}, f32[128,256]{1,0:T(8,128)S(1)}) fusion(f32[256,256]{1,0:T(8,128)} %factor_kernel.1, f32[256,256]{1,0:T(8,128)S(1)} %bitcast.13, s32[]{:T(128)S(6)} %select_n.3), kind=kOutput, calls=%fused_computation.3 | convolution fusion | flops 100696064 | bytes 655364 | tf_op jit(solution)/shard_map/dot_general | solution.py:245
  129.0 0.0 copy-done.1
  129.0 1.0 fusion.4
  130.0 0.6 reshape.20
  130.7 0.1 copy.10
  130.7 4.6 %all_to_all.33 = f32[2,64,2,1024]{3,2,1,0:T(2,128)S(1)} all-to-all(f32[2,64,2,1024]{3,2,1,0:T(2,128)S(1)} %bitcast.11), channel_id=1, replica_groups=mesh['z'=8,'x'=8,'core'=2,'col'=8] {'core'}, dimensions={0} | all-to-all | bytes 2097152 | tf_op jit(solution)/shard_map/all_to_all | solution.py:251
  135.3 0.9 reduce_sum.28
  136.3 21.7 %all_to_all.34 = f32[64,2,1024]{2,1,0:T(2,128)S(1)} all-to-all(f32[64,2,1024]{2,1,0:T(2,128)S(1)} %reduce_sum.28), channel_id=1, replica_groups=mesh['z'=8,'x'=8,'core'=2,'col'=8] {'z','x'}, dimensions={0} | all-to-all | bytes 1048576 | tf_op jit(solution)/shard_map/all_to_all | solution.py:251
  158.0 0.8 reduce_sum.29
  (1 shorter events, 0.0 us)
Async XLA Ops:
  0.6 1.2 copy-start
  20.1 22.5 %all-to-all-start.1 = ((f32[16,16,256]{2,1,0:T(8,128)}), f32[16,16,256]{2,1,0:T(8,128)S(1)}, u32[]{:S(2)}, u32[]{:S(2)}) async-start(f32[16,16,256]{2,1,0:T(8,128)} %broadcast_in_dim.2), calls=%async_computation.1 | async-start | bytes 524288 | tf_op jit(solution)/shard_map/all_to_all | solution.py:251
  42.6 0.7 copy-start.2
  92.9 6.7 %copy-start.4 = (f32[64,8,128]{2,1,0:T(8,128)}, f32[64,8,128]{2,1,0:T(8,128)S(1)}, u32[]{:S(2)}) copy-start(f32[64,8,128]{2,1,0:T(8,128)S(1)} %all_to_all.32.mine_ref) | copy-start | bytes 786436
  92.9 6.7 %collective-permute-start = (f32[64,8,128]{2,1,0:T(8,128)S(1)}, f32[64,8,128]{2,1,0:T(8,128)S(1)}, u32[]{:S(2)}, u32[]{:S(2)}) collective-permute-start(f32[64,8,128]{2,1,0:T(8,128)S(1)} %all_to_all.32.mine_ref), channel_id=1, source_target_pairs={{0,8},{8,0},{1,9},{9,1},{2,10},{10,2},{3,11},{11,3},{4,12},{12,4},... | collective-permute-start | bytes 786440 | tf_op jit(solution)/shard_map/ppermute | solution.py:270
  98.6 28.3 %copy-start.3 = (f32[16,16,256]{2,1,0:T(8,128)S(1)}, f32[16,16,256]{2,1,0:T(8,128)}, u32[]{:S(2)}) copy-start(f32[16,16,256]{2,1,0:T(8,128)} %copy-done.2) | copy-start | bytes 786436
  99.6 0.7 copy-start.5
  126.9 2.1 %copy-start.1 = (f32[128,1024]{1,0:T(8,128)S(1)}, f32[128,1024]{1,0:T(8,128)}, u32[]{:S(2)}) copy-start(f32[128,1024]{1,0:T(8,128)} %param.2) | copy-start | bytes 1572868
